TPU v7x, 32 devices: a whole 2x2x4 slice. The times are simulated.
32 devices in a mesh: groups: 2 (over x), tensor: 16 (over z, y, core).
Axes of the slice: x: 2, y: 2, z: 4, core: 2. Of those that a mesh axis runs over, the one named last changes fastest.
Arguments:
- residual_in: bfloat16 [1024, 6144], P('groups', 'tensor'), parts along dimension 0
- norm_gain: bfloat16 [6144], P('tensor'), may hold values from 0.099609375 to 1.8984375
- final_gain: bfloat16 [6144], P('tensor'), may hold values from 0.099609375 to 1.8984375
- expert_ids: int32 [1024, 2], P('groups'), parts along dimension 0, may hold values from 0 to 3, all different within a row; in each aligned block of 512 rows (0 to 511, 512 to 1023, ...) at most 384 rows name the same one
- gate_values: float32 [1024, 2], P('groups'), parts along dimension 0, may hold values from 0.2 to 1
- w_gate: bfloat16 [6144, 32768], P(None, 'tensor'), may hold values from -0.078125 to 0.078125
- w_up: bfloat16 [6144, 32768], P(None, 'tensor'), may hold values from -0.078125 to 0.078125
- w_down: bfloat16 [32768, 6144], P('tensor')
- lm_head: bfloat16 [6144, 32768], P(None, 'tensor')
- target_ids: int32 [1024], P('groups'), parts along dimension 0, may hold values from 0 to 32767
- lengths: int32 [16], P('groups'), parts along dimension 0, may hold values from 1 to 64
Outputs:
- masked_logprob: float32 [1024], P(('groups', 'tensor')), parts along dimension 0
There are 2 independent parts, one for each index of `groups`. A program takes and returns all parts, laid end to end along the dimension named above; an argument that names none is the same for every part. Nothing has to cross between parts.
Inputs may be any that keep to these rules, and one draw needn't show every extreme that they name: `expert_ids`: no expert is named by more than 384 tokens of a frontier batch, a bound that some block reaches.
All inputs are finite; a program needn't handle non-finite values.
Results may differ from a plain program's by a relative error of at most 0.0055.
Values may be sent and summed in bfloat16 or wider, within the bound.
No kernel may reach another device: no remote copies, remote signals or barrier semaphores. Data moves between devices by JAX's collectives and lax.ppermute only.
A program may use at most 192 MiB of HBM per device.

v0:
```python
import jax
import jax.numpy as jnp
from jax import lax
from jax.sharding import PartitionSpec as P

D = 6144
EXPERTS = 4
EXP_FF = 8192
TOP = 2
SEQ = 64
CAP = 384
epsilon = 1e-05


def combined_all(array, axis, combine):
    everything = jax.tree.map(lambda part: lax.all_gather(part, axis), array)
    leading = jax.tree.map(lambda part: part[0], everything)

    def hop(k, so_far):
        return combine(so_far, jax.tree.map(lambda part: part[k], everything))

    return lax.fori_loop(1, lax.axis_size(axis), hop, leading)


def slots_of(expert_ids):
    flat_ids = expert_ids.reshape(-1)
    pairs = jnp.arange(flat_ids.shape[0], dtype=jnp.int32)
    before = (pairs[None, :] < pairs[:, None]) & (flat_ids[None, :] == flat_ids[:, None])
    return jnp.sum(before.astype(jnp.int32), axis=1).reshape(expert_ids.shape)


def slot_tokens(expert_ids, slot_index):
    slot_code = (expert_ids * CAP + slot_index).reshape(-1)
    owner = jnp.arange(slot_code.shape[0], dtype=jnp.int32) // TOP
    wanted = jnp.arange(EXPERTS * CAP, dtype=jnp.int32)
    matches = slot_code[None, :] == wanted[:, None]
    return jnp.sum(jnp.where(matches, owner[None, :] + 1, 0), axis=1) - 1


def normalize(values, squares_total, gain_vec):
    return (
        values / jnp.sqrt(squares_total[:, None] / D + epsilon) * gain_vec.astype(jnp.float32)
    ).astype(jnp.bfloat16)


def body(
    residual_in,
    norm_gain,
    final_gain,
    expert_ids,
    gate_values,
    w_gate,
    w_up,
    w_down,
    lm_head,
    target_ids,
    lengths,
):
    tokens, feature_cols = residual_in.shape
    hidden_dev = w_gate.shape[1]
    per_expert = EXP_FF // hidden_dev
    expert_now = lax.axis_index("tensor") // per_expert
    stream = residual_in.astype(jnp.float32)
    in_total = lax.psum(jnp.sum(stream * stream, axis=1), "tensor")
    normed = normalize(stream, in_total, norm_gain)
    slot_index = slots_of(expert_ids)
    token_of = slot_tokens(expert_ids, slot_index)
    zero_bf = jnp.zeros((), jnp.bfloat16)
    own_slots = lax.dynamic_slice_in_dim(token_of, expert_now * CAP, CAP)
    occupied = own_slots >= 0
    safe_index = jnp.maximum(own_slots, 0)
    slot_rows = jnp.where(
        occupied[:, None], lax.all_gather(normed, "tensor", axis=1, tiled=True)[safe_index], zero_bf
    )
    gate_out = jnp.dot(slot_rows, w_gate, preferred_element_type=jnp.float32)
    up_out = jnp.dot(slot_rows, w_up, preferred_element_type=jnp.float32)
    hidden = (jax.nn.silu(gate_out) * up_out).astype(jnp.bfloat16)
    partial_value = jnp.dot(hidden, w_down, preferred_element_type=jnp.float32)
    weight_own = jnp.where(expert_ids == expert_now, gate_values, jnp.zeros_like(gate_values))
    weighted = (
        weight_own[:, 0:1] * partial_value[slot_index[:, 0]]
        + weight_own[:, 1:2] * partial_value[slot_index[:, 1]]
    )
    moe_cols = lax.psum_scatter(weighted, "tensor", scatter_dimension=1, tiled=True)
    mixture = stream + moe_cols
    out_total = lax.psum(jnp.sum(mixture * mixture, axis=1), "tensor")
    normed_out = normalize(mixture, out_total, final_gain)
    vocab_dev = lm_head.shape[1]
    logits = jnp.dot(
        lax.all_gather(normed_out, "tensor", axis=1, tiled=True),
        lm_head,
        preferred_element_type=jnp.float32,
    )
    row_max = jnp.max(logits, axis=1)
    row_total = jnp.sum(jnp.exp(logits - row_max[:, None]), axis=1)
    local_ids = target_ids - lax.axis_index("tensor") * vocab_dev
    vocab_cols = jnp.arange(vocab_dev, dtype=jnp.int32)
    picked = jnp.sum(jnp.where(vocab_cols[None, :] == local_ids[:, None], logits, 0.0), axis=1)

    def joined(earlier, later):
        merged_max = jnp.maximum(earlier[0], later[0])
        merged_total = earlier[1] * jnp.exp(earlier[0] - merged_max) + later[1] * jnp.exp(
            later[0] - merged_max
        )
        return (merged_max, merged_total, earlier[2] + later[2])

    merged_max, merged_total, target_logit = combined_all(
        (row_max, row_total, picked), "tensor", joined
    )
    logprob = target_logit - merged_max - jnp.log(merged_total)
    rows_dev = tokens // lax.axis_size("tensor")
    first_row = lax.axis_index("tensor") * rows_dev
    own_rows = lax.dynamic_slice_in_dim(logprob, first_row, rows_dev)
    position = first_row + jnp.arange(rows_dev, dtype=jnp.int32)
    in_length = position % SEQ < lengths[position // SEQ]
    return jnp.where(in_length, own_rows, jnp.zeros_like(own_rows)).astype(jnp.float32)


def solution(mesh):
    return jax.shard_map(
        body,
        mesh=mesh,
        in_specs=(
            P("groups", "tensor"),
            P("tensor"),
            P("tensor"),
            P("groups", None),
            P("groups", None),
            P(None, "tensor"),
            P(None, "tensor"),
            P("tensor", None),
            P(None, "tensor"),
            P("groups"),
            P("groups"),
        ),
        out_specs=P(("groups", "tensor")),
        check_vma=False,
    )
```

profile of v0, /device:TPU:0, one launch (start us, length us, event | category | flops | bytes accessed | tf_op | source)
XLA Modules:
  0.0 534.1 jit_solution(18296530312608750279)
XLA Ops:
  6.5 1.2 fusion.4
  7.7 34.9 %psum.14 = f32[512]{0:T(512)S(1)} all-reduce(f32[512]{0:T(512)S(1)} %fusion.4), channel_id=1, replica_groups=mesh['groups'=2,'tensor'=16] {'tensor'}, use_global_device_ids=true, to_apply=%region_3.4 | all-reduce | flops 512 | bytes 4096 | tf_op jit(solution)/shard_map/psum | solution.py:64
  43.3 1.9 fusion.6
  45.4 0.8 copy.24
  49.5 0.7 compare_select_fusion.2
  50.2 58.2 %all-gather.9.cloned.1.call-done = bf16[512,6144]{1,0:T(8,128)(2,1)} async-done(((bf16[512,384]{1,0:T(8,128)(2,1)}), bf16[512,6144]{1,0:T(8,128)(2,1)}) %all-gather.9.cloned.1.call-update) | async-done | bytes 6291472 | tf_op jit(solution)/shard_map/all_gather | solution.py:73
  108.4 15.5 %gather_fusion.1 = bf16[384,6144]{1,0:T(8,128)(2,1)} fusion(bf16[512,6144]{1,0:T(8,128)(2,1)} %all-gather.9.cloned.1.call-done, s32[1024]{0:T(1024)S(1)} %pad_clamp_fusion.2), kind=kCustom, calls=%fused_computation.1 | custom fusion | bytes 9438720 | tf_op jit(solution)/shard_map/gather | solution.py:73
  123.9 16.5 %fusion.2 = f32[384,2048]{1,0:T(8,128)S(1)} fusion(bf16[6144,2048]{1,0:T(8,128)(2,1)} %param.18, bf16[384,6144]{1,0:T(8,128)(2,1)} %gather_fusion.1, pred[384]{0:T(512)(128)(4,1)S(1)} %fusion.13), kind=kOutput, calls=%fused_computation.20 | convolution fusion | flops 9666035712 | bytes 33030528 | tf_op jit(solution)/shard_map/dot_general | solution.py:75
  140.4 15.2 %multiply_convert_fusion.clone.4 = bf16[384,2048]{1,0:T(8,128)(2,1)S(1)} fusion(f32[384,2048]{1,0:T(8,128)S(1)} %fusion.2, bf16[6144,2048]{1,0:T(8,128)(2,1)} %param.19, bf16[384,6144]{1,0:T(8,128)(2,1)S(1)} %copy-done.2, pred[384]{0:T(512)(128)(4,1)S(1)} %fusion.13), kind=kOutput, calls=%fused_computation.18.clone.clone.clone.1 | convolution fusion | flops 9670754304 | bytes 34603392 | tf_op jit(solution)/shard_map/dot_general | solution.py:76
  155.6 17.2 %fusion.1 = f32[384,6144]{1,0:T(8,128)} fusion(bf16[2048,6144]{1,0:T(8,128)(2,1)} %param.20, bf16[384,2048]{1,0:T(8,128)(2,1)S(1)} %multiply_convert_fusion.clone.4), kind=kOutput, calls=%fused_computation.19 | convolution fusion | flops 9663676416 | bytes 36175872 | tf_op jit(solution)/shard_map/dot_general | solution.py:78
  172.8 16.3 %gather_fusion.2 = f32[512,6144]{1,0:T(8,128)} fusion(f32[384,6144]{1,0:T(8,128)} %fusion.1, s32[1024]{0:T(1024)S(1)} %get-tuple-element.213), kind=kCustom, calls=%fused_computation.2 | custom fusion | bytes 25167872 | tf_op jit(solution)/shard_map/gather | solution.py:81
  189.0 16.2 %gather_fusion.3 = f32[512,6144]{1,0:T(8,128)} fusion(f32[384,6144]{1,0:T(8,128)} %fusion.1, s32[1024]{0:T(1024)S(1)} %get-tuple-element.212), kind=kCustom, calls=%fused_computation.3 | custom fusion | bytes 25167872 | tf_op jit(solution)/shard_map/gather | solution.py:82
  205.2 14.0 %multiply_add_fusion.1 = f32[512,6144]{1,0:T(8,128)} fusion(f32[512,6144]{1,0:T(8,128)} %gather_fusion.3, f32[512,6144]{1,0:T(8,128)} %gather_fusion.2, f32[512]{0:T(512)S(1)} %bitcast.51, f32[512]{0:T(512)S(1)} %bitcast.50), kind=kLoop, calls=%fused_computation.8 | loop fusion | flops 9437184 | bytes 37752832 | tf_op jit(solution)/shard_map/add | solution.py:81
  219.9 132.4 %reduce-scatter.2.cloned.1.call-done = f32[512,384]{1,0:T(8,128)} async-done(((f32[512,6144]{1,0:T(8,128)}), f32[512,384]{1,0:T(8,128)}) %reduce-scatter.2.cloned.1.call-update) | async-done | bytes 786448 | tf_op jit(solution)/shard_map/reduce_scatter | solution.py:84
  352.3 1.3 multiply_reduce_fusion
  353.6 31.6 %psum.15 = f32[512]{0:T(512)S(1)} all-reduce(f32[512]{0:T(512)S(1)} %multiply_reduce_fusion), channel_id=1, replica_groups=mesh['groups'=2,'tensor'=16] {'tensor'}, use_global_device_ids=true, to_apply=%region_6.7 | all-reduce | flops 512 | bytes 4096 | tf_op jit(solution)/shard_map/psum | solution.py:86
  385.2 2.1 multiply_convert_fusion.1
  388.1 62.3 %all-gather.11.cloned.1.call-done = bf16[512,6144]{1,0:T(8,128)(2,1)} async-done(((bf16[512,384]{1,0:T(8,128)(2,1)}), bf16[512,6144]{1,0:T(8,128)(2,1)}) %all-gather.11.cloned.1.call-update) | async-done | bytes 6291472 | tf_op jit(solution)/shard_map/all_gather | solution.py:90
  450.4 18.6 %fusion.22 = (f32[512]{0:T(512)S(1)}, f32[512,2048]{1,0:T(8,128)S(1)}) fusion(bf16[512,6144]{1,0:T(8,128)(2,1)} %all-gather.11.cloned.1.call-done, bf16[6144,2048]{1,0:T(8,128)(2,1)} %param.21), kind=kOutput, calls=%fused_computation.73 | convolution fusion | flops 12885950464 | bytes 35653632 | tf_op jit(solution)/shard_map/dot_general | solution.py:89
  469.0 1.4 select_reduce_fusion.1
  470.4 18.8 %all-gather.5 = f32[16,1,512]{2,1,0:T(1,128)S(1)} all-gather(f32[1,1,512]{2,1,0:T(1,128)S(1)} %bitcast.49), channel_id=4, replica_groups=mesh['groups'=2,'tensor'=16] {'tensor'}, dimensions={0}, use_global_device_ids=true | all-gather | bytes 34816 | tf_op jit(solution)/shard_map/all_gather | solution.py:16
  489.3 17.5 %all-gather.4 = f32[16,1,512]{2,1,0:T(1,128)S(1)} all-gather(f32[1,1,512]{2,1,0:T(1,128)S(1)} %bitcast.48), channel_id=3, replica_groups=mesh['groups'=2,'tensor'=16] {'tensor'}, dimensions={0}, use_global_device_ids=true | all-gather | bytes 34816 | tf_op jit(solution)/shard_map/all_gather | solution.py:16
  506.8 18.8 %all-gather.3 = f32[16,1,512]{2,1,0:T(1,128)S(1)} all-gather(f32[1,1,512]{2,1,0:T(1,128)S(1)} %bitcast.47), channel_id=2, replica_groups=mesh['groups'=2,'tensor'=16] {'tensor'}, dimensions={0}, use_global_device_ids=true | all-gather | bytes 34816 | tf_op jit(solution)/shard_map/all_gather | solution.py:16
  525.6 1.4 while.19
  (107 shorter events, 6.8 us)
Async XLA Ops:
  6.5 380.9 %copy-start = (s32[8]{0:T(128)S(1)}, s32[8]{0:T(128)}, u32[]{:S(2)}) copy-start(s32[8]{0:T(128)} %param.23) | copy-start | bytes 100
  6.5 101.9 %all-gather.9.cloned.1.call-start = ((), (), s32[]{:S(2)}) async-start(), calls=%async_computation.1 | async-start | bytes 6684672 | tf_op jit(solution)/shard_map/all_gather | solution.py:73
  45.3 307.0 %reduce-scatter.2.cloned.1.call-start = ((), (), s32[]{:S(2)}) async-start(), calls=%async_computation.2 | async-start | bytes 13369344 | tf_op jit(solution)/shard_map/reduce_scatter | solution.py:84
  123.9 16.5 %copy-start.2 = (bf16[384,6144]{1,0:T(8,128)(2,1)S(1)}, bf16[384,6144]{1,0:T(8,128)(2,1)}, u32[]{:S(2)}) copy-start(bf16[384,6144]{1,0:T(8,128)(2,1)} %gather_fusion.1) | copy-start | bytes 14155780
  219.2 0.7 copy-start.4
  219.2 133.1 %copy-start.1 = (bf16[512,384]{1,0:T(8,128)(2,1)S(1)}, bf16[512,384]{1,0:T(8,128)(2,1)}, u32[]{:S(2)}) copy-start(bf16[512,384]{1,0:T(8,128)(2,1)} %param.13) | copy-start | bytes 1179652
  219.2 168.9 %copy-start.3 = (s32[512]{0:T(512)S(1)}, s32[512]{0:T(512)}, u32[]{:S(2)}) copy-start(s32[512]{0:T(512)} %param.22) | copy-start | bytes 6148
  219.2 231.2 %all-gather.11.cloned.1.call-start = ((), (), s32[]{:S(2)}) async-start(), calls=%async_computation.3 | async-start | bytes 6684672 | tf_op jit(solution)/shard_map/all_gather | solution.py:90
Sparse Core Ops, SparseCore 0:
  45.4 62.9 all-gather.8
  219.4 132.9 reduce-scatter.1
  387.5 62.9 all-gather.10
where the time goes:
time: 535 us; the launch traced here: 534 us
  waiting for transfers between devices  253 us (47%)
  blocking collectives  122 us (23%)
  matrix products  67.5 us (13%)
  local copies, waits for them, and re-layouts  51.2 us (10%)
  other arithmetic  26.8 us (5%)
  between operations  13.3 us (2%)
    reduce_scatter x1, waiting for transfers between devices, body(): lax.psum_scatter(weighted, 'tensor', scatter_dimension=1, tiled=True)  132 us
    all_gather x1, waiting for transfers between devices, body(): lax.all_gather(normed_out, 'tensor', axis=1, tiled=True)  62.3 us
    all_gather x1, waiting for transfers between devices, body(): lax.all_gather(normed, 'tensor', axis=1, tiled=True)[safe_index]  58.2 us
    all_gather x3, blocking collectives, combined_all(): everything = jax.tree.map(lambda part: lax.all_gather(part, axis), array)  55.2 us
    psum x1, blocking collectives, body(): in_total = lax.psum(jnp.sum(stream * stream, axis=1), 'tensor')  34.9 us
    psum x1, blocking collectives, body(): out_total = lax.psum(jnp.sum(mixture * mixture, axis=1), 'tensor')  31.6 us
    dot_general x1, matrix products, body(): jnp.dot(lax.all_gather(normed_out, 'tensor', axis=1, tiled=True), lm_head...  18.6 us
    dot_general x1, matrix products, body(): partial_value = jnp.dot(hidden, w_down, preferred_element_type=jnp.float32)  17.2 us
  transfers between devices with their start and end apart: 3, of which 3 were waited for; matrix products, arithmetic and copies ran while one was open for 1% of the time, Pallas kernels for 0%

commit v1 on v0

--- a/solution.py
+++ b/solution.py
@@ -10,6 +10,24 @@
 SEQ = 64
 CAP = 384
 epsilon = 1e-05
+
+
+def collect(array, axis, dim):
+    ways, here, step = (lax.axis_size(axis), lax.axis_index(axis), array.shape[dim])
+    shape = [n * ways if d == dim else n for d, n in enumerate(array.shape)]
+    full = lax.dynamic_update_slice_in_dim(
+        jnp.zeros(shape, array.dtype), array, here * step, axis=dim
+    )
+    going_up = going_down = array
+    for far in range(1, ways // 2 + 1):
+        going_up = lax.ppermute(going_up, axis, [(d, (d + 1) % ways) for d in range(ways)])
+        full = lax.dynamic_update_slice_in_dim(full, going_up, (here - far) % ways * step, axis=dim)
+        if 2 * far < ways:
+            going_down = lax.ppermute(going_down, axis, [(d, (d - 1) % ways) for d in range(ways)])
+            full = lax.dynamic_update_slice_in_dim(
+                full, going_down, (here + far) % ways * step, axis=dim
+            )
+    return full
 
 
 def combined_all(array, axis, combine):
@@ -86,11 +104,7 @@
     out_total = lax.psum(jnp.sum(mixture * mixture, axis=1), "tensor")
     normed_out = normalize(mixture, out_total, final_gain)
     vocab_dev = lm_head.shape[1]
-    logits = jnp.dot(
-        lax.all_gather(normed_out, "tensor", axis=1, tiled=True),
-        lm_head,
-        preferred_element_type=jnp.float32,
-    )
+    logits = jnp.dot(collect(normed_out, "tensor", 1), lm_head, preferred_element_type=jnp.float32)
     row_max = jnp.max(logits, axis=1)
     row_total = jnp.sum(jnp.exp(logits - row_max[:, None]), axis=1)
     local_ids = target_ids - lax.axis_index("tensor") * vocab_dev

time: 535 us -> 559 us (1.045)
  starting transfers between devices: 0.09 us -> 31.6 us
  waiting for transfers between devices: 253 us -> 226 us
  local copies, waits for them, and re-layouts: 51.2 us -> 67.7 us
    all_gather x1 -> x0, waiting for transfers between devices: 62.3 us -> none  [body(): lax.all_gather(normed_out, 'tensor', axis=1, tiled=True)]
    ppermute x0 -> x15, waiting for transfers between devices: none -> 35.8 us  [the longest x8 35.7 us: collect(): lax.ppermute(going_up, axis, [(d, (d + 1) % ways) for d in range(ways)])]
    ppermute x0 -> x15, starting transfers between devices: none -> 31.5 us  [the longest x7 22.1 us: collect(): lax.ppermute(going_down, axis, [(d, (d - 1) % ways) for d in range(ways)])]
    dynamic_update_slice x0 -> x15, local copies, waits for them, and re-layouts: none -> 12.4 us  [the longest x8 6.64 us: collect(): lax.dynamic_update_slice_in_dim(full, going_up, (here - far) % ways * ste...]
  transfers between devices with their start and end apart: 3 -> 17, of which waited for: 3 -> 10; matrix products, arithmetic and copies ran while one was open for 1% -> 3% of each run, Pallas kernels for 0% -> 0%
where the time goes in v1:
time: 559 us; the launch traced here: 555 us
  waiting for transfers between devices  226 us (40%)
  blocking collectives  122 us (22%)
  local copies, waits for them, and re-layouts  67.7 us (12%)
  matrix products  67.7 us (12%)
  starting transfers between devices  31.6 us (6%)
  other arithmetic  25.8 us (5%)
  between operations  13.8 us (2%)
    reduce_scatter x1, waiting for transfers between devices, body(): lax.psum_scatter(weighted, 'tensor', scatter_dimension=1, tiled=True)  132 us
    all_gather x1, waiting for transfers between devices, body(): lax.all_gather(normed, 'tensor', axis=1, tiled=True)[safe_index]  58.2 us
    all_gather x3, blocking collectives, combined_all(): everything = jax.tree.map(lambda part: lax.all_gather(part, axis), array)  55.3 us
    ppermute x8, waiting for transfers between devices, collect(): lax.ppermute(going_up, axis, [(d, (d + 1) % ways) for d in range(ways)])  35.7 us
    psum x1, blocking collectives, body(): in_total = lax.psum(jnp.sum(stream * stream, axis=1), 'tensor')  34.9 us
    psum x1, blocking collectives, body(): out_total = lax.psum(jnp.sum(mixture * mixture, axis=1), 'tensor')  31.6 us
    ppermute x7, starting transfers between devices, collect(): lax.ppermute(going_down, axis, [(d, (d - 1) % ways) for d in range(ways)])  22.1 us
    dot_general x1, matrix products, body(): jnp.dot(collect(normed_out, 'tensor', 1), lm_head, preferred_element_type...  18.8 us
  transfers between devices with their start and end apart: 17, of which 10 were waited for; matrix products, arithmetic and copies ran while one was open for 3% of the time, Pallas kernels for 0%

profile of v1, /device:TPU:0, one launch (start us, length us, event | category | flops | bytes accessed | tf_op | source)
XLA Modules:
  0.0 555.4 jit_solution(1002991630882205076)
XLA Ops:
  7.7 34.9 %psum.14 = f32[512]{0:T(512)S(1)} all-reduce(f32[512]{0:T(512)S(1)} %fusion.4), channel_id=1, replica_groups=mesh['groups'=2,'tensor'=16] {'tensor'}, use_global_device_ids=true, to_apply=%region_3.4 | all-reduce | flops 512 | bytes 4096 | tf_op jit(solution)/shard_map/psum | solution.py:82
  50.2 58.2 %all-gather.8.cloned.1.call-done = bf16[512,6144]{1,0:T(8,128)(2,1)} async-done(((bf16[512,384]{1,0:T(8,128)(2,1)}), bf16[512,6144]{1,0:T(8,128)(2,1)}) %all-gather.8.cloned.1.call-update) | async-done | bytes 6291472 | tf_op jit(solution)/shard_map/all_gather | solution.py:91
  108.4 15.5 %gather_fusion.1 = bf16[384,6144]{1,0:T(8,128)(2,1)} fusion(bf16[512,6144]{1,0:T(8,128)(2,1)} %all-gather.8.cloned.1.call-done, s32[1024]{0:T(1024)S(1)} %pad_clamp_fusion.2), kind=kCustom, calls=%fused_computation.1 | custom fusion | bytes 9438720 | tf_op jit(solution)/shard_map/gather | solution.py:91
  123.9 16.5 %fusion.2 = f32[384,2048]{1,0:T(8,128)S(1)} fusion(bf16[6144,2048]{1,0:T(8,128)(2,1)} %param.18, bf16[384,6144]{1,0:T(8,128)(2,1)} %gather_fusion.1, pred[384]{0:T(512)(128)(4,1)S(1)} %fusion.13), kind=kOutput, calls=%fused_computation.20 | convolution fusion | flops 9666035712 | bytes 33030528 | tf_op jit(solution)/shard_map/dot_general | solution.py:93
  140.5 15.2 %multiply_convert_fusion.clone.4 = bf16[384,2048]{1,0:T(8,128)(2,1)S(1)} fusion(f32[384,2048]{1,0:T(8,128)S(1)} %fusion.2, bf16[6144,2048]{1,0:T(8,128)(2,1)} %param.19, bf16[384,6144]{1,0:T(8,128)(2,1)S(1)} %copy-done.2, pred[384]{0:T(512)(128)(4,1)S(1)} %fusion.13), kind=kOutput, calls=%fused_computation.18.clone.clone.clone.1 | convolution fusion | flops 9670754304 | bytes 34603392 | tf_op jit(solution)/shard_map/dot_general | solution.py:94
  155.7 17.2 %fusion.1 = f32[384,6144]{1,0:T(8,128)} fusion(bf16[2048,6144]{1,0:T(8,128)(2,1)} %param.20, bf16[384,2048]{1,0:T(8,128)(2,1)S(1)} %multiply_convert_fusion.clone.4), kind=kOutput, calls=%fused_computation.19 | convolution fusion | flops 9663676416 | bytes 36175872 | tf_op jit(solution)/shard_map/dot_general | solution.py:96
  172.9 16.3 %gather_fusion.2 = f32[512,6144]{1,0:T(8,128)} fusion(f32[384,6144]{1,0:T(8,128)} %fusion.1, s32[1024]{0:T(1024)S(1)} %get-tuple-element.215), kind=kCustom, calls=%fused_computation.2 | custom fusion | bytes 25167872 | tf_op jit(solution)/shard_map/gather | solution.py:99
  189.2 16.7 %gather_fusion.3 = f32[512,6144]{1,0:T(8,128)} fusion(f32[384,6144]{1,0:T(8,128)} %fusion.1, s32[1024]{0:T(1024)S(1)} %get-tuple-element.214), kind=kCustom, calls=%fused_computation.3 | custom fusion | bytes 25167872 | tf_op jit(solution)/shard_map/gather | solution.py:100
  205.9 14.0 %multiply_add_fusion.1 = f32[512,6144]{1,0:T(8,128)} fusion(f32[512,6144]{1,0:T(8,128)} %gather_fusion.3, f32[512,6144]{1,0:T(8,128)} %gather_fusion.2, f32[512]{0:T(512)S(1)} %bitcast.51, f32[512]{0:T(512)S(1)} %bitcast.50), kind=kLoop, calls=%fused_computation.8 | loop fusion | flops 9437184 | bytes 37752832 | tf_op jit(solution)/shard_map/add | solution.py:99
  220.6 132.5 %reduce-scatter.2.cloned.1.call-done = f32[512,384]{1,0:T(8,128)} async-done(((f32[512,6144]{1,0:T(8,128)}), f32[512,384]{1,0:T(8,128)}) %reduce-scatter.2.cloned.1.call-update) | async-done | bytes 786448 | tf_op jit(solution)/shard_map/reduce_scatter | solution.py:102
  354.4 31.6 %psum.15 = f32[512]{0:T(512)S(1)} all-reduce(f32[512]{0:T(512)S(1)} %multiply_reduce_fusion), channel_id=1, replica_groups=mesh['groups'=2,'tensor'=16] {'tensor'}, use_global_device_ids=true, to_apply=%region_6.7 | all-reduce | flops 512 | bytes 4096 | tf_op jit(solution)/shard_map/psum | solution.py:104
  390.4 4.4 collective-permute-start.1
  394.9 5.5 collective-permute-done
  400.3 4.5 collective-permute-start.3
  404.9 5.5 collective-permute-done.2
  414.9 5.5 collective-permute-done.4
  425.6 4.7 collective-permute-done.6
  430.3 3.8 collective-permute-start.8
  436.5 3.8 collective-permute-done.8
  463.5 6.6 %collective-permute-done.14 = bf16[512,384]{1,0:T(8,128)(2,1)S(1)} collective-permute-done((bf16[512,384]{1,0:T(8,128)(2,1)S(1)}, bf16[512,384]{1,0:T(8,128)(2,1)S(1)}, u32[]{:S(2)}, u32[]{:S(2)}) %collective-permute-start.14) | collective-permute-done | bytes 393248 | tf_op jit(solution)/shard_map/ppermute | solution.py:23
  470.9 18.8 %fusion.22 = (f32[512]{0:T(512)S(1)}, f32[512,2048]{1,0:T(8,128)S(1)}) fusion(bf16[512,6144]{1,0:T(8,128)(2,1)} %constant_dynamic-update-slice_fusion, bf16[6144,2048]{1,0:T(8,128)(2,1)} %param.21), kind=kOutput, calls=%fused_computation.89 | convolution fusion | flops 12885950464 | bytes 35653632 | tf_op jit(solution)/shard_map/dot_general | solution.py:107
  491.1 19.0 %all-gather.5 = f32[16,1,512]{2,1,0:T(1,128)S(1)} all-gather(f32[1,1,512]{2,1,0:T(1,128)S(1)} %bitcast.49), channel_id=4, replica_groups=mesh['groups'=2,'tensor'=16] {'tensor'}, dimensions={0}, use_global_device_ids=true | all-gather | bytes 34816 | tf_op jit(solution)/shard_map/all_gather | solution.py:34
  510.1 17.5 %all-gather.4 = f32[16,1,512]{2,1,0:T(1,128)S(1)} all-gather(f32[1,1,512]{2,1,0:T(1,128)S(1)} %bitcast.48), channel_id=3, replica_groups=mesh['groups'=2,'tensor'=16] {'tensor'}, dimensions={0}, use_global_device_ids=true | all-gather | bytes 34816 | tf_op jit(solution)/shard_map/all_gather | solution.py:34
  527.6 18.8 %all-gather.3 = f32[16,1,512]{2,1,0:T(1,128)S(1)} all-gather(f32[1,1,512]{2,1,0:T(1,128)S(1)} %bitcast.47), channel_id=2, replica_groups=mesh['groups'=2,'tensor'=16] {'tensor'}, dimensions={0}, use_global_device_ids=true | all-gather | bytes 34816 | tf_op jit(solution)/shard_map/all_gather | solution.py:34
  (152 shorter events, 55.5 us)
Async XLA Ops:
  6.5 418.4 %copy-start = (s32[8]{0:T(128)S(1)}, s32[8]{0:T(128)}, u32[]{:S(2)}) copy-start(s32[8]{0:T(128)} %param.23) | copy-start | bytes 100
  6.5 101.9 %all-gather.8.cloned.1.call-start = ((), (), s32[]{:S(2)}) async-start(), calls=%async_computation.1 | async-start | bytes 6684672 | tf_op jit(solution)/shard_map/all_gather | solution.py:91
  45.3 307.8 %reduce-scatter.2.cloned.1.call-start = ((), (), s32[]{:S(2)}) async-start(), calls=%async_computation.2 | async-start | bytes 13369344 | tf_op jit(solution)/shard_map/reduce_scatter | solution.py:102
  123.9 16.5 %copy-start.2 = (bf16[384,6144]{1,0:T(8,128)(2,1)S(1)}, bf16[384,6144]{1,0:T(8,128)(2,1)}, u32[]{:S(2)}) copy-start(bf16[384,6144]{1,0:T(8,128)(2,1)} %gather_fusion.1) | copy-start | bytes 14155780
  219.9 0.7 copy-start.5
  219.9 133.1 %copy-start.1 = (bf16[512,384]{1,0:T(8,128)(2,1)S(1)}, bf16[512,384]{1,0:T(8,128)(2,1)}, u32[]{:S(2)}) copy-start(bf16[512,384]{1,0:T(8,128)(2,1)} %param.13) | copy-start | bytes 1179652
  219.9 214.2 %copy-start.4 = (s32[512]{0:T(512)S(1)}, s32[512]{0:T(512)}, u32[]{:S(2)}) copy-start(s32[512]{0:T(512)} %param.22) | copy-start | bytes 6148
  353.0 36.4 %copy-start.3 = (f32[512,384]{1,0:T(8,128)S(1)}, f32[512,384]{1,0:T(8,128)}, u32[]{:S(2)}) copy-start(f32[512,384]{1,0:T(8,128)} %reduce-scatter.2.cloned.1.call-done) | copy-start | bytes 2359300
  390.4 9.9 %collective-permute-start = (bf16[512,384]{1,0:T(8,128)(2,1)S(1)}, bf16[512,384]{1,0:T(8,128)(2,1)S(1)}, u32[]{:S(2)}, u32[]{:S(2)}) collective-permute-start(bf16[512,384]{1,0:T(8,128)(2,1)S(1)} %get-tuple-element.207), channel_id=1, source_target_pairs={{0,1},{1,2},{2,3},{3,4},{4,5},{5,6},{6,7},{7,8},{8,9},{9,10},{10,1... | collective-permute-start | bytes 1179656 | tf_op jit(solution)/shard_map/ppermute | solution.py:23
  390.4 9.9 %collective-permute-start.1 = (bf16[512,384]{1,0:T(8,128)(2,1)S(1)}, bf16[512,384]{1,0:T(8,128)(2,1)S(1)}, u32[]{:S(2)}, u32[]{:S(2)}) collective-permute-start(bf16[512,384]{1,0:T(8,128)(2,1)S(1)} %get-tuple-element.207), channel_id=1, source_target_pairs={{0,15},{1,0},{2,1},{3,2},{4,3},{5,4},{6,5},{7,6},{8,7},{9,8},{10,9... | collective-permute-start | bytes 1179656 | tf_op jit(solution)/shard_map/ppermute | solution.py:26
  400.3 10.0 %collective-permute-start.2 = (bf16[512,384]{1,0:T(8,128)(2,1)S(1)}, bf16[512,384]{1,0:T(8,128)(2,1)S(1)}, u32[]{:S(2)}, u32[]{:S(2)}) collective-permute-start(bf16[512,384]{1,0:T(8,128)(2,1)S(1)} %collective-permute-done), channel_id=1, source_target_pairs={{0,1},{1,2},{2,3},{3,4},{4,5},{5,6},{6,7},{7,8},{8,9},{9,10},{10,1... | collective-permute-start | bytes 1179656 | tf_op jit(solution)/shard_map/ppermute | solution.py:23
  400.3 11.0 %collective-permute-start.3 = (bf16[512,384]{1,0:T(8,128)(2,1)S(1)}, bf16[512,384]{1,0:T(8,128)(2,1)S(1)}, u32[]{:S(2)}, u32[]{:S(2)}) collective-permute-start(bf16[512,384]{1,0:T(8,128)(2,1)S(1)} %collective-permute-done.1), channel_id=1, source_target_pairs={{0,15},{1,0},{2,1},{3,2},{4,3},{5,4},{6,5},{7,6},{8,7},{9,8},{10,9... | collective-permute-start | bytes 1179656 | tf_op jit(solution)/shard_map/ppermute | solution.py:26
  410.3 10.0 %collective-permute-start.4 = (bf16[512,384]{1,0:T(8,128)(2,1)S(1)}, bf16[512,384]{1,0:T(8,128)(2,1)S(1)}, u32[]{:S(2)}, u32[]{:S(2)}) collective-permute-start(bf16[512,384]{1,0:T(8,128)(2,1)S(1)} %collective-permute-done.2), channel_id=1, source_target_pairs={{0,1},{1,2},{2,3},{3,4},{4,5},{5,6},{6,7},{7,8},{8,9},{9,10},{10,1... | collective-permute-start | bytes 1179656 | tf_op jit(solution)/shard_map/ppermute | solution.py:23
  411.3 11.4 %collective-permute-start.5 = (bf16[512,384]{1,0:T(8,128)(2,1)S(1)}, bf16[512,384]{1,0:T(8,128)(2,1)S(1)}, u32[]{:S(2)}, u32[]{:S(2)}) collective-permute-start(bf16[512,384]{1,0:T(8,128)(2,1)S(1)} %collective-permute-done.3), channel_id=1, source_target_pairs={{0,15},{1,0},{2,1},{3,2},{4,3},{5,4},{6,5},{7,6},{8,7},{9,8},{10,9... | collective-permute-start | bytes 1179656 | tf_op jit(solution)/shard_map/ppermute | solution.py:26
  420.3 10.0 %collective-permute-start.6 = (bf16[512,384]{1,0:T(8,128)(2,1)S(1)}, bf16[512,384]{1,0:T(8,128)(2,1)S(1)}, u32[]{:S(2)}, u32[]{:S(2)}) collective-permute-start(bf16[512,384]{1,0:T(8,128)(2,1)S(1)} %collective-permute-done.4), channel_id=1, source_target_pairs={{0,1},{1,2},{2,3},{3,4},{4,5},{5,6},{6,7},{7,8},{8,9},{9,10},{10,1... | collective-permute-start | bytes 1179656 | tf_op jit(solution)/shard_map/ppermute | solution.py:23
  422.8 12.2 %collective-permute-start.7 = (bf16[512,384]{1,0:T(8,128)(2,1)S(1)}, bf16[512,384]{1,0:T(8,128)(2,1)S(1)}, u32[]{:S(2)}, u32[]{:S(2)}) collective-permute-start(bf16[512,384]{1,0:T(8,128)(2,1)S(1)} %collective-permute-done.5), channel_id=1, source_target_pairs={{0,15},{1,0},{2,1},{3,2},{4,3},{5,4},{6,5},{7,6},{8,7},{9,8},{10,9... | collective-permute-start | bytes 1179656 | tf_op jit(solution)/shard_map/ppermute | solution.py:26
  430.3 9.9 %collective-permute-start.8 = (bf16[512,384]{1,0:T(8,128)(2,1)S(1)}, bf16[512,384]{1,0:T(8,128)(2,1)S(1)}, u32[]{:S(2)}, u32[]{:S(2)}) collective-permute-start(bf16[512,384]{1,0:T(8,128)(2,1)S(1)} %collective-permute-done.6), channel_id=1, source_target_pairs={{0,1},{1,2},{2,3},{3,4},{4,5},{5,6},{6,7},{7,8},{8,9},{9,10},{10,1... | collective-permute-start | bytes 1179656 | tf_op jit(solution)/shard_map/ppermute | solution.py:23
  435.0 8.9 %collective-permute-start.9 = (bf16[512,384]{1,0:T(8,128)(2,1)S(1)}, bf16[512,384]{1,0:T(8,128)(2,1)S(1)}, u32[]{:S(2)}, u32[]{:S(2)}) collective-permute-start(bf16[512,384]{1,0:T(8,128)(2,1)S(1)} %collective-permute-done.7), channel_id=1, source_target_pairs={{0,15},{1,0},{2,1},{3,2},{4,3},{5,4},{6,5},{7,6},{8,7},{9,8},{10,9... | collective-permute-start | bytes 1179656 | tf_op jit(solution)/shard_map/ppermute | solution.py:26
  440.2 10.0 %collective-permute-start.10 = (bf16[512,384]{1,0:T(8,128)(2,1)S(1)}, bf16[512,384]{1,0:T(8,128)(2,1)S(1)}, u32[]{:S(2)}, u32[]{:S(2)}) collective-permute-start(bf16[512,384]{1,0:T(8,128)(2,1)S(1)} %collective-permute-done.8), channel_id=1, source_target_pairs={{0,1},{1,2},{2,3},{3,4},{4,5},{5,6},{6,7},{7,8},{8,9},{9,10},{10,1... | collective-permute-start | bytes 1179656 | tf_op jit(solution)/shard_map/ppermute | solution.py:23
  443.9 10.0 %collective-permute-start.11 = (bf16[512,384]{1,0:T(8,128)(2,1)S(1)}, bf16[512,384]{1,0:T(8,128)(2,1)S(1)}, u32[]{:S(2)}, u32[]{:S(2)}) collective-permute-start(bf16[512,384]{1,0:T(8,128)(2,1)S(1)} %collective-permute-done.9), channel_id=1, source_target_pairs={{0,15},{1,0},{2,1},{3,2},{4,3},{5,4},{6,5},{7,6},{8,7},{9,8},{10,9... | collective-permute-start | bytes 1179656 | tf_op jit(solution)/shard_map/ppermute | solution.py:26
  450.2 10.0 %collective-permute-start.12 = (bf16[512,384]{1,0:T(8,128)(2,1)S(1)}, bf16[512,384]{1,0:T(8,128)(2,1)S(1)}, u32[]{:S(2)}, u32[]{:S(2)}) collective-permute-start(bf16[512,384]{1,0:T(8,128)(2,1)S(1)} %collective-permute-done.10), channel_id=1, source_target_pairs={{0,1},{1,2},{2,3},{3,4},{4,5},{5,6},{6,7},{7,8},{8,9},{9,10},{10,1... | collective-permute-start | bytes 1179656 | tf_op jit(solution)/shard_map/ppermute | solution.py:23
  453.8 8.9 %collective-permute-start.13 = (bf16[512,384]{1,0:T(8,128)(2,1)S(1)}, bf16[512,384]{1,0:T(8,128)(2,1)S(1)}, u32[]{:S(2)}, u32[]{:S(2)}) collective-permute-start(bf16[512,384]{1,0:T(8,128)(2,1)S(1)} %collective-permute-done.11), channel_id=1, source_target_pairs={{0,15},{1,0},{2,1},{3,2},{4,3},{5,4},{6,5},{7,6},{8,7},{9,8},{10,9... | collective-permute-start | bytes 1179656 | tf_op jit(solution)/shard_map/ppermute | solution.py:26
  460.2 9.9 %collective-permute-start.14 = (bf16[512,384]{1,0:T(8,128)(2,1)S(1)}, bf16[512,384]{1,0:T(8,128)(2,1)S(1)}, u32[]{:S(2)}, u32[]{:S(2)}) collective-permute-start(bf16[512,384]{1,0:T(8,128)(2,1)S(1)} %collective-permute-done.12), channel_id=1, source_target_pairs={{0,1},{1,2},{2,3},{3,4},{4,5},{5,6},{6,7},{7,8},{8,9},{9,10},{10,1... | collective-permute-start | bytes 1179656 | tf_op jit(solution)/shard_map/ppermute | solution.py:23
Sparse Core Ops, SparseCore 0:
  45.4 62.9 all-gather.7
  220.1 132.9 reduce-scatter.1
